TPU v7x, 32 devices: a whole 2x2x4 slice. The times are simulated.
32 devices in a mesh: node: 4 (over z), dom: 8 (over y, x, core).
Axes of the slice: x: 2, y: 2, z: 4, core: 2. Of those that a mesh axis runs over, the one named last changes fastest.
Arguments:
- probes: float32 [32, 16, 16, 128], P(None, 'dom'), may hold values from -24 to 24
- slope: float32 [16, 16, 128], P('dom'), may hold values from 4 to 6
- root: float32 [16, 16, 128], P('dom'), may hold values from 0.3 to 0.7
- damping: float32 [16, 16, 128], P('dom'), may hold values from 0.3 to 1.2
Outputs:
- moments: float32 [2, 2, 32, 16, 16, 128], P(None, None, 'node', 'dom')
- projections: float32 [2, 2, 32, 32], replicated
All inputs are finite; a program needn't handle non-finite values.
Results may differ from a plain program's by a relative error of at most 0.00013.
Values sent between devices are 32-bit elements; how exact they have to be, the bound alone decides.
A program may use at most 64 MiB of HBM per device.

v0:
```python
import math
import jax
import jax.numpy as jnp
from jax import lax
from jax.sharding import PartitionSpec as P

NODE_DEV = 2
SWEEPS = 8
CENTRE = 0.5
RADIUS = 2.0


def grid_step(source, fields, factor_re, factor_im):
    padded = jnp.pad(fields, ((0, 0), (0, 0), (1, 1), (1, 1), (1, 1)))
    total = padded[:, :, 2:, 1:-1, 1:-1] + padded[:, :, :-2, 1:-1, 1:-1]
    total = total + padded[:, :, 1:-1, 2:, 1:-1] + padded[:, :, 1:-1, :-2, 1:-1]
    total = total + padded[:, :, 1:-1, 1:-1, 2:] + padded[:, :, 1:-1, 1:-1, :-2]
    real_part = source + total[:, 0]
    imag_part = total[:, 1]
    return jnp.stack(
        [
            real_part * factor_re - imag_part * factor_im,
            real_part * factor_im + imag_part * factor_re,
        ],
        axis=1,
    )


def inverse_diagonal(shift_real, shift_imaginary, slope, root, damping, guard):
    zr_col = shift_real[:, None, None, None, None]
    zi_col = shift_imaginary[:, None, None, None, None]
    decay = jnp.exp(-zr_col)
    real_d = slope * (zr_col - root) + damping * (decay * jnp.cos(zi_col))
    imag_d = slope * zi_col - damping * (decay * jnp.sin(zi_col))
    scale = 1.0 / (real_d * real_d + imag_d * imag_d + guard)
    return (real_d * scale, -imag_d * scale)


def per_system(fields, weight_re, weight_im):
    a_col = weight_re[:, None, None, None]
    b_col = weight_im[:, None, None, None]
    return jnp.stack(
        [a_col * fields[:, 0] - b_col * fields[:, 1], a_col * fields[:, 1] + b_col * fields[:, 0]]
    )


def body(probes, slope, root, damping):
    vectors = probes.shape[0]
    planes = probes.shape[1]
    groups = lax.axis_size("node")
    total = NODE_DEV * groups
    first = (lax.axis_index("node") * NODE_DEV).astype(jnp.float32)
    dom_size = lax.axis_size("dom")
    count = NODE_DEV * vectors // dom_size
    replicated = jnp.broadcast_to(probes[None], (NODE_DEV,) + probes.shape).reshape(
        (NODE_DEV * vectors,) + probes.shape[1:]
    )
    own = lax.all_to_all(replicated, "dom", split_axis=0, concat_axis=1, tiled=True)
    slope_all, root_all, damping_all = (
        lax.all_gather(slope, "dom", axis=0, tiled=True),
        lax.all_gather(root, "dom", axis=0, tiled=True),
        lax.all_gather(damping, "dom", axis=0, tiled=True),
    )
    system = lax.axis_index("dom") * count + jnp.arange(count)
    position = first + (system // vectors).astype(jnp.float32)
    theta = 2.0 * math.pi * (position + 0.5) / total
    shift_real = CENTRE + RADIUS * jnp.cos(theta)
    shift_imaginary = RADIUS * jnp.sin(theta)
    qre, qim = inverse_diagonal(
        shift_real, shift_imaginary, slope_all[None], root_all[None], damping_all[None], 0.0
    )
    qre = qre[:, 0]
    qim = qim[:, 0]
    fields = jnp.stack([own * qre, own * qim], axis=1)
    for sweep in range(SWEEPS):
        fields = grid_step(own, fields, qre, qim)
    weight_re = RADIUS * jnp.cos(theta) / total
    weight_im = RADIUS * jnp.sin(theta) / total
    shifted_re = weight_re * shift_real - weight_im * shift_imaginary
    shifted_im = weight_re * shift_imaginary + weight_im * shift_real
    terms = jnp.stack(
        [per_system(fields, weight_re, weight_im), per_system(fields, shifted_re, shifted_im)]
    )
    back = lax.all_to_all(terms, "dom", split_axis=3, concat_axis=2, tiled=True)
    local = jnp.sum(back.reshape((2, 2, NODE_DEV, vectors) + probes.shape[1:]), axis=2)
    flat = local.reshape(4 * vectors, -1)
    basis = probes.reshape(vectors, -1)
    partial_value = lax.dot_general(
        flat,
        basis,
        (((1,), (1,)), ((), ())),
        precision=lax.Precision.HIGHEST,
        preferred_element_type=jnp.float32,
    )
    cells = planes * probes.shape[2] * probes.shape[3] * lax.axis_size("dom")
    projections = lax.psum(partial_value.reshape(2, 2, vectors, vectors) / cells, ("node", "dom"))
    summed = lax.psum(local, "node")
    share = vectors // groups
    moments = lax.dynamic_slice_in_dim(summed, lax.axis_index("node") * share, share, 2)
    return (moments, projections)


def solution(mesh):
    in_specs = (
        P(None, "dom", None, None),
        P("dom", None, None),
        P("dom", None, None),
        P("dom", None, None),
    )
    out_specs = (P(None, None, "node", "dom", None, None), P())
    return jax.shard_map(body, mesh=mesh, in_specs=in_specs, out_specs=out_specs, check_vma=False)
```

profile of v0, /device:TPU:0, one launch (start us, length us, event | category | flops | bytes accessed | tf_op | source)
XLA Modules:
  0.0 260.8 jit_solution(6893673430703613702)
XLA Ops:
  7.2 0.0 copy-start.2
  7.2 0.0 copy-start.3
  7.2 0.0 copy-start.4
  7.2 2.2 broadcast_in_dim.2
  9.4 5.2 %all-to-all-start = ((f32[64,2,16,128]{3,2,1,0:T(8,128)}), f32[64,2,16,128]{3,2,1,0:T(8,128)S(1)}, u32[]{:S(2)}, u32[]{:S(2)}) async-start(f32[64,2,16,128]{3,2,1,0:T(8,128)} %bitcast), calls=%async_computation | async-start | bytes 2097152 | tf_op jit(solution)/shard_map/all_to_all | solution.py:58
  14.6 0.0 copy-done.2
  14.6 18.8 %all_gather.9 = f32[16,16,128]{2,1,0:T(8,128)S(1)} all-gather(f32[2,16,128]{2,1,0:T(8,128)S(1)} %copy-done.2), channel_id=1, replica_groups=mesh['node'=4,'dom'=8] {'dom'}, dimensions={0}, use_global_device_ids=true | all-gather | bytes 147456 | tf_op jit(solution)/shard_map/all_gather | solution.py:60
  33.4 0.0 copy-done.3
  33.4 8.3 %all_gather.10 = f32[16,16,128]{2,1,0:T(8,128)S(1)} all-gather(f32[2,16,128]{2,1,0:T(8,128)S(1)} %copy-done.3), channel_id=1, replica_groups=mesh['node'=4,'dom'=8] {'dom'}, dimensions={0}, use_global_device_ids=true | all-gather | bytes 147456 | tf_op jit(solution)/shard_map/all_gather | solution.py:61
  41.7 0.0 copy-done.4
  41.7 9.1 %all_gather.11 = f32[16,16,128]{2,1,0:T(8,128)S(1)} all-gather(f32[2,16,128]{2,1,0:T(8,128)S(1)} %copy-done.4), channel_id=1, replica_groups=mesh['node'=4,'dom'=8] {'dom'}, dimensions={0}, use_global_device_ids=true | all-gather | bytes 147456 | tf_op jit(solution)/shard_map/all_gather | solution.py:62
  50.8 0.1 multiply_subtract_fusion.12
  50.9 0.0 all-to-all-done
  50.9 0.1 copy.15
  51.0 0.6 fusion.19
  51.6 2.6 select_maximum_fusion.7
  54.2 3.3 %slice_add_fusion.35 = f32[8,2,16,16,128]{4,3,2,0,1:T(8,128)S(1)} fusion(f32[8,2,18,18,130]{4,3,2,0,1:T(8,128)S(1)} %select_maximum_fusion.7), kind=kLoop, calls=%fused_computation.56 | loop fusion | flops 2621440 | bytes 14680064 | tf_op jit(solution)/shard_map/add | solution.py:17
  57.5 0.8 multiply_subtract_fusion.10
  58.3 2.4 select_maximum_fusion.6
  60.7 3.3 %slice_add_fusion.30 = f32[8,2,16,16,128]{4,3,2,0,1:T(8,128)S(1)} fusion(f32[8,2,18,18,130]{4,3,2,0,1:T(8,128)S(1)} %select_maximum_fusion.6), kind=kLoop, calls=%fused_computation.51 | loop fusion | flops 2621440 | bytes 14680064 | tf_op jit(solution)/shard_map/add | solution.py:17
  63.9 0.8 multiply_subtract_fusion.9
  64.7 2.4 select_maximum_fusion.5
  67.1 3.3 %slice_add_fusion.25 = f32[8,2,16,16,128]{4,3,2,0,1:T(8,128)S(1)} fusion(f32[8,2,18,18,130]{4,3,2,0,1:T(8,128)S(1)} %select_maximum_fusion.5), kind=kLoop, calls=%fused_computation.46 | loop fusion | flops 2621440 | bytes 14680064 | tf_op jit(solution)/shard_map/add | solution.py:17
  70.4 0.8 multiply_subtract_fusion.8
  71.2 2.4 select_maximum_fusion.4
  73.6 3.3 %slice_add_fusion.20 = f32[8,2,16,16,128]{4,3,2,0,1:T(8,128)S(1)} fusion(f32[8,2,18,18,130]{4,3,2,0,1:T(8,128)S(1)} %select_maximum_fusion.4), kind=kLoop, calls=%fused_computation.41 | loop fusion | flops 2621440 | bytes 14680064 | tf_op jit(solution)/shard_map/add | solution.py:17
  76.8 0.8 multiply_subtract_fusion.7
  77.6 2.6 select_maximum_fusion.3
  80.2 3.3 %slice_add_fusion.15 = f32[8,2,16,16,128]{4,3,2,0,1:T(8,128)S(1)} fusion(f32[8,2,18,18,130]{4,3,2,0,1:T(8,128)S(1)} %select_maximum_fusion.3), kind=kLoop, calls=%fused_computation.36 | loop fusion | flops 2621440 | bytes 14680064 | tf_op jit(solution)/shard_map/add | solution.py:17
  83.5 0.8 multiply_subtract_fusion.6
  84.3 2.4 select_maximum_fusion.2
  86.7 3.3 %slice_add_fusion.10 = f32[8,2,16,16,128]{4,3,2,0,1:T(8,128)S(1)} fusion(f32[8,2,18,18,130]{4,3,2,0,1:T(8,128)S(1)} %select_maximum_fusion.2), kind=kLoop, calls=%fused_computation.31 | loop fusion | flops 2621440 | bytes 14680064 | tf_op jit(solution)/shard_map/add | solution.py:17
  90.0 0.8 multiply_subtract_fusion.5
  90.8 2.4 select_maximum_fusion.1
  93.1 3.3 %slice_add_fusion.5 = f32[8,2,16,16,128]{4,3,2,0,1:T(8,128)S(1)} fusion(f32[8,2,18,18,130]{4,3,2,0,1:T(8,128)S(1)} %select_maximum_fusion.1), kind=kLoop, calls=%fused_computation.26 | loop fusion | flops 2621440 | bytes 14680064 | tf_op jit(solution)/shard_map/add | solution.py:17
  96.4 0.8 multiply_subtract_fusion.4
  97.2 2.4 select_maximum_fusion
  99.6 3.5 %slice_add_fusion = f32[8,2,16,16,128]{4,3,2,0,1:T(8,128)S(1)} fusion(f32[8,2,18,18,130]{4,3,2,0,1:T(8,128)S(1)} %select_maximum_fusion), kind=kLoop, calls=%fused_computation.21 | loop fusion | flops 2621440 | bytes 14680064 | tf_op jit(solution)/shard_map/add | solution.py:17
  103.1 0.9 multiply_subtract_fusion.1
  104.1 0.5 multiply_subtract_fusion
  104.6 0.4 maximum_bitcast_fusion
  105.0 0.4 pad_maximum_fusion
  105.4 0.6 copy.17
  106.0 51.6 %all_to_all.36 = f32[2,2,8,16,16,128]{5,4,2,1,0,3:T(8,128)S(1)} all-to-all(f32[2,2,8,16,16,128]{5,4,2,1,0,3:T(8,128)S(1)} %copy.17), channel_id=1, replica_groups=mesh['node'=4,'dom'=8] {'dom'}, dimensions={3} | all-to-all | bytes 8388608 | tf_op jit(solution)/shard_map/all_to_all | solution.py:84
  157.6 0.5 copy.19
  158.2 0.0 copy-start.1
  158.2 0.5 bitcast_reduce_fusion
  158.7 0.0 copy-start
  158.7 0.5 copy-done.1
  159.2 3.1 %fusion.10 = f32[2,2,32,32]{3,2,1,0:T(8,128)S(1)} fusion(f32[2,2,32,2,16,128]{5,4,3,2,1,0:T(8,128)S(1)} %bitcast_reduce_fusion, f32[32,2,16,128,1,1]{3,2,1,0,5,4:T(8,128)S(1)} %bitcast.53), kind=kOutput, calls=%fused_computation.66 | convolution fusion | flops 201330688 | bytes 2637824 | tf_op jit(solution)/shard_map/dot_general | solution.py:88
  162.3 0.0 all-reduce.10.cloned.1.call-start
  162.4 0.0 copy-done
  162.4 0.7 all-reduce.10.cloned.1.call-update
  163.1 42.9 %psum.15 = f32[2,2,32,32]{3,2,1,0:T(8,128)} all-reduce(f32[2,2,32,32]{3,2,1,0:T(8,128)S(1)} %fusion.10), channel_id=1, replica_groups=mesh['node'=4,'dom'=8] {'node','dom'}, use_global_device_ids=true, to_apply=%region_2.3 | all-reduce | flops 4096 | bytes 32768 | tf_op jit(solution)/shard_map/psum | solution.py:96
  206.0 46.1 %all-reduce.10.cloned.1.call-done = f32[2,2,32,2,16,128]{5,4,3,2,1,0:T(8,128)} async-done(((f32[2,2,32,2,16,128]{5,4,3,2,1,0:T(8,128)}), f32[2,2,32,2,16,128]{5,4,3,2,1,0:T(8,128)}) %all-reduce.10.cloned.1.call-update) | async-done | bytes 2097168 | tf_op jit(solution)/shard_map/psum | solution.py:97
  252.1 1.9 constant_dynamic-slice_fusion
  (1 shorter events, 0.0 us)
Async XLA Ops:
  7.2 7.4 %copy-start.2 = (f32[2,16,128]{2,1,0:T(8,128)S(1)}, f32[2,16,128]{2,1,0:T(8,128)}, u32[]{:S(2)}) copy-start(f32[2,16,128]{2,1,0:T(8,128)} %param.5) | copy-start | bytes 49156
  7.2 26.2 %copy-start.3 = (f32[2,16,128]{2,1,0:T(8,128)S(1)}, f32[2,16,128]{2,1,0:T(8,128)}, u32[]{:S(2)}) copy-start(f32[2,16,128]{2,1,0:T(8,128)} %param.6) | copy-start | bytes 49156
  7.2 34.5 %copy-start.4 = (f32[2,16,128]{2,1,0:T(8,128)S(1)}, f32[2,16,128]{2,1,0:T(8,128)}, u32[]{:S(2)}) copy-start(f32[2,16,128]{2,1,0:T(8,128)} %param.7) | copy-start | bytes 49156
  9.4 41.5 %all-to-all-start = ((f32[64,2,16,128]{3,2,1,0:T(8,128)}), f32[64,2,16,128]{3,2,1,0:T(8,128)S(1)}, u32[]{:S(2)}, u32[]{:S(2)}) async-start(f32[64,2,16,128]{3,2,1,0:T(8,128)} %bitcast), calls=%async_computation | async-start | bytes 2097152 | tf_op jit(solution)/shard_map/all_to_all | solution.py:58
  158.2 1.0 copy-start.1
  158.7 3.6 %copy-start = (f32[2,2,32,2,16,128]{5,4,3,2,1,0:T(8,128)}, f32[2,2,32,2,16,128]{5,4,3,2,1,0:T(8,128)S(1)}, u32[]{:S(2)}) copy-start(f32[2,2,32,2,16,128]{5,4,3,2,1,0:T(8,128)S(1)} %bitcast_reduce_fusion) | copy-start | bytes 6291460
  162.3 89.8 %all-reduce.10.cloned.1.call-start = ((), (), s32[]{:S(2)}) async-start(), calls=%async_computation.2 | async-start | bytes 4194304 | tf_op jit(solution)/shard_map/psum | solution.py:97
Sparse Core Ops, SparseCore 0:
  165.5 86.5 all-reduce.9
where the time goes:
time: 261 us
  blocking collectives  131 us (50%)
  other arithmetic  54.8 us (21%)
  waiting for transfers between devices  46.8 us (18%)
  between operations  14.3 us (5%)
  local copies, waits for them, and re-layouts  5.8 us (2%)
  starting transfers between devices  5.24 us (2%)
  matrix products  3.08 us (1%)
    all_to_all x1, blocking collectives, body(): back = lax.all_to_all(terms, 'dom', split_axis=3, concat_axis=2, tiled=True)  51.6 us
    psum x1, waiting for transfers between devices, body(): summed = lax.psum(local, 'node')  46.1 us
    psum x1, blocking collectives, body(): lax.psum(partial_value.reshape(2, 2, vectors, vectors) / cells, ('node',...  42.9 us
    add x8, other arithmetic, grid_step(): total = total + padded[:, :, 1:-1, 1:-1, 2:] + padded[:, :, 1:-1, 1:-1, :-2]  26.4 us
    all_gather x1, blocking collectives, body(): lax.all_gather(slope, 'dom', axis=0, tiled=True)  18.8 us
    another operation x7, other arithmetic, grid_step(): jnp.stack([real_part * factor_re - imag_part * factor_im, real_part * fac...  16.9 us
    all_gather x1, blocking collectives, body(): lax.all_gather(damping, 'dom', axis=0, tiled=True)  9.1 us
    all_gather x1, blocking collectives, body(): lax.all_gather(root, 'dom', axis=0, tiled=True)  8.31 us
  transfers between devices with their start and end apart: 2, of which 1 were waited for; matrix products, arithmetic and copies ran while one was open for 0% of the time, Pallas kernels for 0%

commit v1 on v0

--- a/solution.py
+++ b/solution.py
@@ -94,7 +94,7 @@
     )
     cells = planes * probes.shape[2] * probes.shape[3] * lax.axis_size("dom")
     projections = lax.psum(partial_value.reshape(2, 2, vectors, vectors) / cells, ("node", "dom"))
-    summed = lax.psum(local, "node")
+    summed = jnp.sum(lax.all_gather(local, "node"), axis=0)
     share = vectors // groups
     moments = lax.dynamic_slice_in_dim(summed, lax.axis_index("node") * share, share, 2)
     return (moments, projections)

time: 261 us -> 323 us (1.24)
  waiting for transfers between devices: 46.8 us -> 96.1 us
  other arithmetic: 54.8 us -> 60.9 us
  blocking collectives: 131 us -> 137 us
    all_gather x0 -> x1, waiting for transfers between devices: none -> 96.1 us  [body(): summed = jnp.sum(lax.all_gather(local, 'node'), axis=0)]
    psum x1 -> x0, waiting for transfers between devices: 46.1 us -> none  [body(): summed = lax.psum(local, 'node')]
    psum x1, blocking collectives: 42.9 us -> 49.5 us  [body(): lax.psum(partial_value.reshape(2, 2, vectors, vectors) / cells, ('node',...]
    reduce_sum x0 -> x1, other arithmetic: none -> 4.64 us  [body(): summed = jnp.sum(lax.all_gather(local, 'node'), axis=0)]
  transfers between devices with their start and end apart: 2 -> 2, of which waited for: 1 -> 1; matrix products, arithmetic and copies ran while one was open for 0% -> 1% of each run, Pallas kernels for 0% -> 0%
where the time goes in v1:
time: 323 us
  blocking collectives  137 us (42%)
  waiting for transfers between devices  96.1 us (30%)
  other arithmetic  60.9 us (19%)
  between operations  14.3 us (4%)
  local copies, waits for them, and re-layouts  5.8 us (2%)
  starting transfers between devices  5.24 us (2%)
    all_gather x1, waiting for transfers between devices, body(): summed = jnp.sum(lax.all_gather(local, 'node'), axis=0)  96.1 us
    all_to_all x1, blocking collectives, body(): back = lax.all_to_all(terms, 'dom', split_axis=3, concat_axis=2, tiled=True)  51.6 us
    psum x1, blocking collectives, body(): lax.psum(partial_value.reshape(2, 2, vectors, vectors) / cells, ('node',...  49.5 us
    add x8, other arithmetic, grid_step(): total = total + padded[:, :, 1:-1, 1:-1, 2:] + padded[:, :, 1:-1, 1:-1, :-2]  26.4 us
    all_gather x1, blocking collectives, body(): lax.all_gather(slope, 'dom', axis=0, tiled=True)  18.8 us
    another operation x7, other arithmetic, grid_step(): jnp.stack([real_part * factor_re - imag_part * factor_im, real_part * fac...  16.9 us
    all_gather x1, blocking collectives, body(): lax.all_gather(damping, 'dom', axis=0, tiled=True)  9.1 us
    all_gather x1, blocking collectives, body(): lax.all_gather(root, 'dom', axis=0, tiled=True)  8.31 us
  transfers between devices with their start and end apart: 2, of which 1 were waited for; matrix products, arithmetic and copies ran while one was open for 1% of the time, Pallas kernels for 0%

profile of v1, /device:TPU:0, one launch (start us, length us, event | category | flops | bytes accessed | tf_op | source)
XLA Modules:
  0.0 322.7 jit_solution(3880006488031442775)
XLA Ops:
  7.2 0.0 copy-start.2
  7.2 0.0 copy-start.3
  7.2 0.0 copy-start.4
  7.2 2.2 broadcast_in_dim.2
  9.4 5.2 %all-to-all-start = ((f32[64,2,16,128]{3,2,1,0:T(8,128)}), f32[64,2,16,128]{3,2,1,0:T(8,128)S(1)}, u32[]{:S(2)}, u32[]{:S(2)}) async-start(f32[64,2,16,128]{3,2,1,0:T(8,128)} %bitcast), calls=%async_computation | async-start | bytes 2097152 | tf_op jit(solution)/shard_map/all_to_all | solution.py:58
  14.6 0.0 all-gather.3.cloned.1.call-start
  14.6 0.0 copy-done.2
  14.6 18.8 %all_gather.15 = f32[16,16,128]{2,1,0:T(8,128)S(1)} all-gather(f32[2,16,128]{2,1,0:T(8,128)S(1)} %copy-done.2), channel_id=1, replica_groups=mesh['node'=4,'dom'=8] {'dom'}, dimensions={0}, use_global_device_ids=true | all-gather | bytes 147456 | tf_op jit(solution)/shard_map/all_gather | solution.py:60
  33.4 0.0 copy-done.3
  33.4 8.3 %all_gather.16 = f32[16,16,128]{2,1,0:T(8,128)S(1)} all-gather(f32[2,16,128]{2,1,0:T(8,128)S(1)} %copy-done.3), channel_id=1, replica_groups=mesh['node'=4,'dom'=8] {'dom'}, dimensions={0}, use_global_device_ids=true | all-gather | bytes 147456 | tf_op jit(solution)/shard_map/all_gather | solution.py:61
  41.7 0.0 copy-done.4
  41.7 9.1 %all_gather.17 = f32[16,16,128]{2,1,0:T(8,128)S(1)} all-gather(f32[2,16,128]{2,1,0:T(8,128)S(1)} %copy-done.4), channel_id=1, replica_groups=mesh['node'=4,'dom'=8] {'dom'}, dimensions={0}, use_global_device_ids=true | all-gather | bytes 147456 | tf_op jit(solution)/shard_map/all_gather | solution.py:62
  50.8 0.1 multiply_subtract_fusion.12
  50.9 0.0 all-to-all-done
  50.9 0.1 copy.12
  51.0 0.6 fusion.19
  51.6 2.6 select_maximum_fusion.7
  54.2 3.3 %slice_add_fusion.35 = f32[8,2,16,16,128]{4,3,2,0,1:T(8,128)S(1)} fusion(f32[8,2,18,18,130]{4,3,2,0,1:T(8,128)S(1)} %select_maximum_fusion.7), kind=kLoop, calls=%fused_computation.56 | loop fusion | flops 2621440 | bytes 14680064 | tf_op jit(solution)/shard_map/add | solution.py:17
  57.5 0.8 multiply_subtract_fusion.10
  58.3 2.4 select_maximum_fusion.6
  60.7 3.3 %slice_add_fusion.30 = f32[8,2,16,16,128]{4,3,2,0,1:T(8,128)S(1)} fusion(f32[8,2,18,18,130]{4,3,2,0,1:T(8,128)S(1)} %select_maximum_fusion.6), kind=kLoop, calls=%fused_computation.51 | loop fusion | flops 2621440 | bytes 14680064 | tf_op jit(solution)/shard_map/add | solution.py:17
  63.9 0.8 multiply_subtract_fusion.9
  64.7 2.4 select_maximum_fusion.5
  67.1 3.3 %slice_add_fusion.25 = f32[8,2,16,16,128]{4,3,2,0,1:T(8,128)S(1)} fusion(f32[8,2,18,18,130]{4,3,2,0,1:T(8,128)S(1)} %select_maximum_fusion.5), kind=kLoop, calls=%fused_computation.46 | loop fusion | flops 2621440 | bytes 14680064 | tf_op jit(solution)/shard_map/add | solution.py:17
  70.4 0.8 multiply_subtract_fusion.8
  71.2 2.4 select_maximum_fusion.4
  73.6 3.3 %slice_add_fusion.20 = f32[8,2,16,16,128]{4,3,2,0,1:T(8,128)S(1)} fusion(f32[8,2,18,18,130]{4,3,2,0,1:T(8,128)S(1)} %select_maximum_fusion.4), kind=kLoop, calls=%fused_computation.41 | loop fusion | flops 2621440 | bytes 14680064 | tf_op jit(solution)/shard_map/add | solution.py:17
  76.8 0.8 multiply_subtract_fusion.7
  77.6 2.6 select_maximum_fusion.3
  80.2 3.3 %slice_add_fusion.15 = f32[8,2,16,16,128]{4,3,2,0,1:T(8,128)S(1)} fusion(f32[8,2,18,18,130]{4,3,2,0,1:T(8,128)S(1)} %select_maximum_fusion.3), kind=kLoop, calls=%fused_computation.36 | loop fusion | flops 2621440 | bytes 14680064 | tf_op jit(solution)/shard_map/add | solution.py:17
  83.5 0.8 multiply_subtract_fusion.6
  84.3 2.4 select_maximum_fusion.2
  86.7 3.3 %slice_add_fusion.10 = f32[8,2,16,16,128]{4,3,2,0,1:T(8,128)S(1)} fusion(f32[8,2,18,18,130]{4,3,2,0,1:T(8,128)S(1)} %select_maximum_fusion.2), kind=kLoop, calls=%fused_computation.31 | loop fusion | flops 2621440 | bytes 14680064 | tf_op jit(solution)/shard_map/add | solution.py:17
  90.0 0.8 multiply_subtract_fusion.5
  90.7 2.4 select_maximum_fusion.1
  93.1 3.3 %slice_add_fusion.5 = f32[8,2,16,16,128]{4,3,2,0,1:T(8,128)S(1)} fusion(f32[8,2,18,18,130]{4,3,2,0,1:T(8,128)S(1)} %select_maximum_fusion.1), kind=kLoop, calls=%fused_computation.26 | loop fusion | flops 2621440 | bytes 14680064 | tf_op jit(solution)/shard_map/add | solution.py:17
  96.4 0.8 multiply_subtract_fusion.4
  97.2 2.4 select_maximum_fusion
  99.6 3.5 %slice_add_fusion = f32[8,2,16,16,128]{4,3,2,0,1:T(8,128)S(1)} fusion(f32[8,2,18,18,130]{4,3,2,0,1:T(8,128)S(1)} %select_maximum_fusion), kind=kLoop, calls=%fused_computation.21 | loop fusion | flops 2621440 | bytes 14680064 | tf_op jit(solution)/shard_map/add | solution.py:17
  103.1 0.9 multiply_subtract_fusion.1
  104.1 0.5 multiply_subtract_fusion
  104.5 0.4 maximum_bitcast_fusion
  105.0 0.4 pad_maximum_fusion
  105.5 0.6 copy.14
  106.1 51.6 %all_to_all.36 = f32[2,2,8,16,16,128]{5,4,2,1,0,3:T(8,128)S(1)} all-to-all(f32[2,2,8,16,16,128]{5,4,2,1,0,3:T(8,128)S(1)} %copy.14), channel_id=1, replica_groups=mesh['node'=4,'dom'=8] {'dom'}, dimensions={3} | all-to-all | bytes 8388608 | tf_op jit(solution)/shard_map/all_to_all | solution.py:84
  157.6 0.5 copy.16
  158.2 0.0 copy-start.1
  158.2 1.9 bitcast_reduce_fusion
  160.1 0.0 copy-start
  160.1 0.0 all-gather.3.cloned.1.call-update
  160.2 0.0 copy-done.1
  160.2 1.6 copy-done
  161.7 3.1 fusion.10
  164.8 49.5 %psum.7 = f32[2,2,32,32]{3,2,1,0:T(8,128)} all-reduce(f32[2,2,32,32]{3,2,1,0:T(8,128)S(1)} %fusion.10), channel_id=1, replica_groups=mesh['node'=4,'dom'=8] {'node','dom'}, use_global_device_ids=true, to_apply=%region_2.3 | all-reduce | flops 4096 | bytes 32768 | tf_op jit(solution)/shard_map/psum | solution.py:96
  214.3 96.1 %all-gather.3.cloned.1.call-done = f32[8,2,32,2,16,128]{5,4,3,2,1,0:T(8,128)} async-done(((f32[2,2,32,2,16,128]{5,4,3,2,1,0:T(8,128)}), f32[8,2,32,2,16,128]{5,4,3,2,1,0:T(8,128)}) %all-gather.3.cloned.1.call-update) | async-done | bytes 8388624 | tf_op jit(solution)/shard_map/all_gather | solution.py:97
  310.3 4.6 %reduce_sum.19 = f32[2,2,32,2,16,128]{5,4,3,2,1,0:T(8,128)S(1)} reduce(f32[4,2,2,32,2,16,128]{6,5,4,3,2,1,0:T(8,128)} %bitcast.53, f32[]{:T(128)} %constant.49.clone.1), dimensions={0}, to_apply=%region_1.2 | reduce | flops 1572864 | bytes 10485764 | tf_op jit(solution)/shard_map/reduce_sum | solution.py:97
  315.0 0.8 constant_dynamic-slice_fusion
  (1 shorter events, 0.0 us)
Async XLA Ops:
  7.2 7.5 %copy-start.2 = (f32[2,16,128]{2,1,0:T(8,128)S(1)}, f32[2,16,128]{2,1,0:T(8,128)}, u32[]{:S(2)}) copy-start(f32[2,16,128]{2,1,0:T(8,128)} %param.5) | copy-start | bytes 49156
  7.2 26.2 %copy-start.3 = (f32[2,16,128]{2,1,0:T(8,128)S(1)}, f32[2,16,128]{2,1,0:T(8,128)}, u32[]{:S(2)}) copy-start(f32[2,16,128]{2,1,0:T(8,128)} %param.6) | copy-start | bytes 49156
  7.2 34.5 %copy-start.4 = (f32[2,16,128]{2,1,0:T(8,128)S(1)}, f32[2,16,128]{2,1,0:T(8,128)}, u32[]{:S(2)}) copy-start(f32[2,16,128]{2,1,0:T(8,128)} %param.7) | copy-start | bytes 49156
  9.4 41.5 %all-to-all-start = ((f32[64,2,16,128]{3,2,1,0:T(8,128)}), f32[64,2,16,128]{3,2,1,0:T(8,128)S(1)}, u32[]{:S(2)}, u32[]{:S(2)}) async-start(f32[64,2,16,128]{3,2,1,0:T(8,128)} %bitcast), calls=%async_computation | async-start | bytes 2097152 | tf_op jit(solution)/shard_map/all_to_all | solution.py:58
  14.6 295.8 %all-gather.3.cloned.1.call-start = ((), (), s32[]{:S(2)}) async-start(), calls=%async_computation.2 | async-start | bytes 10485760 | tf_op jit(solution)/shard_map/all_gather | solution.py:97
  158.2 2.0 copy-start.1
  160.1 1.6 copy-start
Sparse Core Ops, SparseCore 0:
  160.3 150.0 all-gather.2
